TPU v7x, 32 devices: a whole 2x2x4 slice. The times are simulated.
32 devices in a mesh: groups: 2 (over y), mp: 4 (over z), dp: 2 (over x), guide: 2 (over core).
Axes of the slice: x: 2, y: 2, z: 4, core: 2. Of those that a mesh axis runs over, the one named last changes fastest.
Arguments:
- tokens: bfloat16 [192, 8192], P(('groups', 'mp'), ('dp', 'guide')), parts along dimension 0, may hold values from -6 to 6
- w_gate: bfloat16 [8192, 14336], P(('dp', 'guide'), 'mp'), may hold values from -0.0625 to 0.0625
- w_up: bfloat16 [8192, 14336], P(('dp', 'guide'), 'mp'), may hold values from -0.0625 to 0.0625
- w_down: bfloat16 [14336, 8192], P('mp', ('dp', 'guide')), may hold values from -0.046875 to 0.046875
Outputs:
- layer_output: bfloat16 [192, 8192], P(('groups', 'mp'), ('dp', 'guide')), parts along dimension 0
There are 2 independent parts, one for each index of `groups`. A program takes and returns all parts, laid end to end along the dimension named above; an argument that names none is the same for every part. Nothing has to cross between parts.
All inputs are finite; a program needn't handle non-finite values.
Results may differ from a plain program's by a relative error of at most 0.0049.
Values may be sent and summed in bfloat16 or wider, within the bound.
A program may use at most 128 MiB of HBM per device.

v0:
```python
import jax
import jax.numpy as jnp
from jax import lax
from jax.sharding import PartitionSpec as P


def per_device(tokens, w_gate, w_up, w_down):
    columns = w_gate.shape[1]
    paired_weights = jnp.concatenate([w_gate, w_up], axis=1)
    partial_terms = jnp.dot(
        lax.all_gather(tokens, "mp", axis=0, tiled=True),
        paired_weights,
        preferred_element_type=jnp.float32,
    )
    summed = lax.psum_scatter(partial_terms, ("dp", "guide"), scatter_dimension=0, tiled=True)
    hidden_share = (jax.nn.silu(summed[:, :columns]) * summed[:, columns:]).astype(jnp.bfloat16)
    hidden = lax.all_gather(hidden_share, ("dp", "guide"), axis=0, tiled=True)
    output_share = lax.psum_scatter(
        jnp.dot(hidden, w_down, preferred_element_type=jnp.float32),
        "mp",
        scatter_dimension=0,
        tiled=True,
    )
    return output_share.astype(jnp.bfloat16)


def solution(mesh):
    placed = (
        P(("groups", "mp"), ("dp", "guide")),
        P(("dp", "guide"), "mp"),
        P(("dp", "guide"), "mp"),
        P("mp", ("dp", "guide")),
    )
    return jax.shard_map(
        per_device,
        mesh=mesh,
        in_specs=placed,
        out_specs=P(("groups", "mp"), ("dp", "guide")),
        check_vma=False,
    )
```

profile of v0, /device:TPU:0, one launch (start us, length us, event | category | flops | bytes accessed | tf_op | source)
XLA Modules:
  0.0 122.6 jit_solution(6414061938836751330)
XLA Ops:
  6.5 0.0 reduce-scatter.3.cloned.1.call-start
  6.5 16.5 %all_gather.6 = bf16[96,2048]{1,0:T(8,128)(2,1)S(1)} all-gather(bf16[24,2048]{1,0:T(8,128)(2,1)} %param.4), channel_id=1, replica_groups=mesh['groups'=2,'mp'=4,'dp'=2,'guide'=2] {'mp'}, dimensions={0}, use_global_device_ids=true | all-gather | bytes 491520 | tf_op jit(solution)/shard_map/all_gather | solution.py:11
  23.0 12.8 %fusion.4 = f32[96,7168]{1,0:T(8,128)} fusion(bf16[96,2048]{1,0:T(8,128)(2,1)S(1)} %all_gather.6, bf16[2048,3584]{1,0:T(8,128)(2,1)} %param.6, bf16[2048,3584]{1,0:T(8,128)(2,1)} %param.5), kind=kOutput, calls=%fused_computation.4 | convolution fusion | flops 2877292544 | bytes 32505856 | tf_op jit(solution)/shard_map/dot_general | solution.py:10
  35.8 0.0 reduce-scatter.3.cloned.1.call-update
  35.8 0.0 reduce-scatter.5.cloned.1.call-start
  35.8 37.2 %reduce-scatter.3.cloned.1.call-done = f32[24,7168]{1,0:T(8,128)} async-done(((f32[96,7168]{1,0:T(8,128)}), f32[24,7168]{1,0:T(8,128)}) %reduce-scatter.3.cloned.1.call-update) | async-done | bytes 688144 | tf_op jit(solution)/shard_map/reduce_scatter | solution.py:15
  73.0 1.2 fusion.7
  74.2 7.5 %all_gather.7 = bf16[96,3584]{1,0:T(8,128)(2,1)S(1)} all-gather(bf16[24,3584]{1,0:T(8,128)(2,1)S(1)} %fusion.7), channel_id=1, replica_groups=mesh['groups'=2,'mp'=4,'dp'=2,'guide'=2] {'dp','guide'}, dimensions={0}, use_global_device_ids=true | all-gather | bytes 860160 | tf_op jit(solution)/shard_map/all_gather | solution.py:17
  81.7 8.7 %fusion.9 = f32[96,2048]{1,0:T(8,128)} fusion(bf16[96,3584]{1,0:T(8,128)(2,1)S(1)} %all_gather.7, bf16[3584,2048]{1,0:T(8,128)(2,1)} %param.7), kind=kOutput, calls=%fused_computation.8 | convolution fusion | flops 1409286144 | bytes 16154624 | tf_op jit(solution)/shard_map/dot_general | solution.py:19
  90.4 0.0 reduce-scatter.5.cloned.1.call-update
  90.4 23.8 %reduce-scatter.5.cloned.1.call-done = f32[24,2048]{1,0:T(8,128)} async-done(((f32[96,2048]{1,0:T(8,128)}), f32[24,2048]{1,0:T(8,128)}) %reduce-scatter.5.cloned.1.call-update) | async-done | bytes 196624 | tf_op jit(solution)/shard_map/reduce_scatter | solution.py:18
  114.2 1.6 %convert_element_type.7 = bf16[24,2048]{1,0:T(8,128)(2,1)} convert(f32[24,2048]{1,0:T(8,128)} %reduce-scatter.5.cloned.1.call-done) | non-fusion elementwise | flops 49152 | bytes 294912 | tf_op jit(solution)/shard_map/convert_element_type | solution.py:24
Async XLA Ops:
  6.5 66.5 %reduce-scatter.3.cloned.1.call-start = ((), (), s32[]{:S(2)}) async-start(), calls=%async_computation.2 | async-start | bytes 3440640 | tf_op jit(solution)/shard_map/reduce_scatter | solution.py:15
  35.8 78.4 %reduce-scatter.5.cloned.1.call-start = ((), (), s32[]{:S(2)}) async-start(), calls=%async_computation.3 | async-start | bytes 983040 | tf_op jit(solution)/shard_map/reduce_scatter | solution.py:18
Sparse Core Ops, SparseCore 0:
  35.9 37.0 reduce-scatter.2
  90.5 23.6 reduce-scatter.4
where the time goes:
time: 123 us
  waiting for transfers between devices  61.1 us (50%)
  blocking collectives  24 us (20%)
  matrix products  21.4 us (17%)
  between operations  13.4 us (11%)
  other arithmetic  2.76 us (2%)
    reduce_scatter x1, waiting for transfers between devices, per_device(): lax.psum_scatter(partial_terms, ('dp', 'guide'), scatter_dimension=0, til...  37.2 us
    reduce_scatter x1, waiting for transfers between devices, per_device(): lax.psum_scatter(jnp.dot(hidden, w_down, preferred_element_type=jnp.float...  23.8 us
    all_gather x1, blocking collectives, per_device(): lax.all_gather(tokens, 'mp', axis=0, tiled=True)  16.5 us
    dot_general x1, matrix products, per_device(): jnp.dot(lax.all_gather(tokens, 'mp', axis=0, tiled=True), paired_weights,...  12.8 us
    dot_general x1, matrix products, per_device(): jnp.dot(hidden, w_down, preferred_element_type=jnp.float32)  8.66 us
    all_gather x1, blocking collectives, per_device(): hidden = lax.all_gather(hidden_share, ('dp', 'guide'), axis=0, tiled=True)  7.49 us
  transfers between devices with their start and end apart: 2, of which 2 were waited for; matrix products, arithmetic and copies ran while one was open for 0% of the time, Pallas kernels for 0%

commit v1 on v0

v1 whole, which is shorter than its diff:
```python
import functools

import jax
import jax.numpy as jnp
from jax import lax
from jax.experimental import pallas as pl
from jax.experimental.pallas import tpu as pltpu
from jax.sharding import PartitionSpec as P

MESH = pl.DeviceIdType.MESH
F32, BF16 = jnp.float32, jnp.bfloat16
WIDTH = 256
OUT_WIDTH = 512


def kernel(mp, dp, tokens, w_gate, w_up, w_down, out, *scratch):
    (gate_v, up_v, down_v, tok_in, tok_f, tok, sum1_out, sum1_in, total, kept, sum2_out, sum2_in,
     hid, part, out_kept, out_send, out_recv,
     w_sem, down_sem, tok_own, tok_s, tok_r, s1_s, s1_r, s2_s, s2_r, hx_s, hx_r, hp_s, hp_r, c_s, c_r) = scratch
    m, d, g = lax.axis_index("mp"), lax.axis_index("dp"), lax.axis_index("guide")
    rows = tokens.shape[0]
    n_half = gate_v.shape[0] // 2
    n_out = down_v.shape[0]
    share = rows * mp // dp
    other = 1 - g

    def weights(side, c):
        half = other if side == 0 else g
        cols = pl.ds(pl.multiple_of((half * n_half + c) * WIDTH, WIDTH), WIDTH)
        slot = side * n_half + c
        return (pltpu.make_async_copy(w_gate.at[:, cols], gate_v.at[slot], w_sem.at[0, slot]),
                pltpu.make_async_copy(w_up.at[:, cols], up_v.at[slot], w_sem.at[1, slot]))

    def downs(n):
        return pltpu.make_async_copy(
            w_down.at[:, pl.ds(pl.multiple_of(n * OUT_WIDTH, OUT_WIDTH), OUT_WIDTH)], down_v.at[n], down_sem.at[n])

    own = pltpu.make_async_copy(tokens, tok_in.at[m], tok_own)
    own.start()
    for side in range(2):
        @pl.loop(0, n_half)
        def _(c):
            for copy in weights(side, c):
                copy.start()

    @pl.loop(0, n_out)
    def _(n):
        downs(n).start()

    barrier = pltpu.get_barrier_semaphore()
    for j in range(1, mp):
        pl.semaphore_signal(barrier, inc=1, device_id={"mp": lax.rem(m + j, mp)}, device_id_type=MESH)
    for j in range(1, dp):
        pl.semaphore_signal(barrier, inc=1, device_id={"dp": lax.rem(d + j, dp)}, device_id_type=MESH)
    pl.semaphore_signal(barrier, inc=1, device_id={"guide": other}, device_id_type=MESH)
    pl.semaphore_wait(barrier, mp + dp - 1)

    def tok_copy(j):
        return pltpu.make_async_remote_copy(
            src_ref=tokens, dst_ref=tok_in.at[m], send_sem=tok_s.at[j - 1], recv_sem=tok_r.at[j - 1],
            device_id={"mp": lax.rem(m + j, mp)}, device_id_type=MESH)

    for j in range(mp - 1, 0, -1):
        tok_copy(j).start()
    own.wait()
    for j in range(1, mp):
        tok_copy(j).wait_recv()
    for q in range(mp):
        tok_f[q * rows:(q + 1) * rows, :] = tok_in[q].astype(F32)
    tok[...] = tok_f[...].astype(BF16)

    def s1_copy(c):
        return pltpu.make_async_remote_copy(
            src_ref=sum1_out.at[c], dst_ref=sum1_in.at[c], send_sem=s1_s.at[c], recv_sem=s1_r.at[c],
            device_id={"guide": other}, device_id_type=MESH)

    @pl.loop(0, n_half)
    def _(c):
        for copy in weights(0, c):
            copy.wait()
        sum1_out[c, 0] = jnp.dot(tok[...], gate_v[c], preferred_element_type=F32).astype(BF16)
        sum1_out[c, 1] = jnp.dot(tok[...], up_v[c], preferred_element_type=F32).astype(BF16)
        s1_copy(c).start()

    def s2_copy(c, j):
        return pltpu.make_async_remote_copy(
            src_ref=sum2_out.at[c, j - 1], dst_ref=sum2_in.at[c, j - 1],
            send_sem=s2_s.at[c, j - 1], recv_sem=s2_r.at[c, j - 1],
            device_id={"dp": lax.rem(d + j, dp)}, device_id_type=MESH)

    def rows_of(b):
        return pl.ds(pl.multiple_of(b * share, 16), share)

    @pl.loop(0, n_half)
    def _(c):
        for copy in weights(1, c):
            copy.wait()
        total[0] = jnp.dot(tok[...], gate_v[n_half + c], preferred_element_type=F32)
        total[1] = jnp.dot(tok[...], up_v[n_half + c], preferred_element_type=F32)
        s1_copy(c).wait_recv()
        for j in range(1, dp):
            b = rows_of(lax.rem(d + j, dp))
            for k in range(2):
                sum2_out[c, j - 1, k] = (total[k, b, :] + sum1_in[c, k, b, :].astype(F32)).astype(BF16)
            s2_copy(c, j).start()
        for k in range(2):
            kept[c, k] = total[k, rows_of(d), :] + sum1_in[c, k, rows_of(d), :].astype(F32)

    def block(b, half, c):
        return hid.at[rows_of(b), pl.ds(pl.multiple_of((half * n_half + c) * WIDTH, WIDTH), WIDTH)]

    def hx_copy(c, j):
        return pltpu.make_async_remote_copy(
            src_ref=block(d, g, c), dst_ref=block(d, g, c), send_sem=hx_s.at[c, j - 1], recv_sem=hx_r.at[c, j - 1],
            device_id={"dp": lax.rem(d + j, dp)}, device_id_type=MESH)

    def hp_copy(c, j):
        b = block(lax.rem(d + dp - j, dp), g, c)
        return pltpu.make_async_remote_copy(
            src_ref=b, dst_ref=b, send_sem=hp_s.at[c, j], recv_sem=hp_r.at[c, j],
            device_id={"guide": other}, device_id_type=MESH)

    @pl.loop(0, n_half)
    def _(c):
        for j in range(1, dp):
            s2_copy(c, j).wait_recv()
        gate, up = kept[c, 0], kept[c, 1]
        for j in range(1, dp):
            gate = gate + sum2_in[c, j - 1, 0].astype(F32)
            up = up + sum2_in[c, j - 1, 1].astype(F32)
        block(d, g, c)[...] = (gate / (1.0 + jnp.exp(-gate)) * up).astype(BF16)
        for j in range(1, dp):
            hx_copy(c, j).start()
        hp_copy(c, 0).start()

    @pl.loop(0, n_half)
    def _(c):
        for j in range(1, dp):
            hx_copy(c, j).wait_recv()
            hp_copy(c, j).start()

    @pl.loop(0, n_half)
    def _(c):
        for j in range(dp):
            hp_copy(c, j).wait_recv()

    def c_copy(n, j):
        return pltpu.make_async_remote_copy(
            src_ref=out_send.at[n, j - 1], dst_ref=out_recv.at[n, j - 1],
            send_sem=c_s.at[n, j - 1], recv_sem=c_r.at[n, j - 1],
            device_id={"mp": lax.rem(m + j, mp)}, device_id_type=MESH)

    def out_rows(q):
        return pl.ds(pl.multiple_of(q * rows, 8), rows)

    @pl.loop(0, n_out)
    def _(n):
        downs(n).wait()
        part[...] = jnp.dot(hid[...], down_v[n], preferred_element_type=F32)
        for j in range(mp - 1, 0, -1):
            out_send[n, j - 1] = part[out_rows(lax.rem(m + j, mp)), :].astype(BF16)
            c_copy(n, j).start()
        out_kept[n] = part[out_rows(m), :]

    for n in range(n_out):
        acc = out_kept[n]
        for j in range(1, mp):
            c_copy(n, j).wait_recv()
            acc = acc + out_recv[n, j - 1].astype(F32)
        out[:, n * OUT_WIDTH:(n + 1) * OUT_WIDTH] = acc.astype(BF16)

    for j in range(1, mp):
        tok_copy(j).wait_send()

    @pl.loop(0, n_half)
    def _(c):
        s1_copy(c).wait_send()
        for j in range(1, dp):
            s2_copy(c, j).wait_send()
            hx_copy(c, j).wait_send()
        for j in range(dp):
            hp_copy(c, j).wait_send()

    @pl.loop(0, n_out)
    def _(n):
        for j in range(1, mp):
            c_copy(n, j).wait_send()


def fused(mp, dp, tokens, w_gate, w_up, w_down):
    rows, depth = tokens.shape
    cols, wide = w_gate.shape[1], w_down.shape[1]
    nc, nh, no = cols // WIDTH, cols // WIDTH // 2, wide // OUT_WIDTH
    full, share = rows * mp, rows * mp // dp
    dma = pltpu.SemaphoreType.DMA
    any_, vmem = pl.BlockSpec(memory_space=pl.ANY), pl.BlockSpec(memory_space=pltpu.VMEM)
    return pl.pallas_call(
        functools.partial(kernel, mp, dp),
        out_shape=jax.ShapeDtypeStruct((rows, wide), BF16),
        in_specs=[any_] * 4,
        out_specs=vmem,
        scratch_shapes=[
            pltpu.VMEM((nc, depth, WIDTH), BF16),
            pltpu.VMEM((nc, depth, WIDTH), BF16),
            pltpu.VMEM((no, cols, OUT_WIDTH), BF16),
            pltpu.VMEM((mp, rows, depth), BF16),
            pltpu.VMEM((full, depth), F32),
            pltpu.VMEM((full, depth), BF16),
            pltpu.VMEM((nh, 2, full, WIDTH), BF16),
            pltpu.VMEM((nh, 2, full, WIDTH), BF16),
            pltpu.VMEM((2, full, WIDTH), F32),
            pltpu.VMEM((nh, 2, share, WIDTH), F32),
            pltpu.VMEM((nh, dp - 1, 2, share, WIDTH), BF16),
            pltpu.VMEM((nh, dp - 1, 2, share, WIDTH), BF16),
            pltpu.VMEM((full, cols), BF16),
            pltpu.VMEM((full, OUT_WIDTH), F32),
            pltpu.VMEM((no, rows, OUT_WIDTH), F32),
            pltpu.VMEM((no, mp - 1, rows, OUT_WIDTH), BF16),
            pltpu.VMEM((no, mp - 1, rows, OUT_WIDTH), BF16),
            dma((2, nc)), dma((no,)), dma, dma((mp - 1,)), dma((mp - 1,)),
            dma((nh,)), dma((nh,)), dma((nh, dp - 1)), dma((nh, dp - 1)),
            dma((nh, dp - 1)), dma((nh, dp - 1)), dma((nh, dp)), dma((nh, dp)),
            dma((no, mp - 1)), dma((no, mp - 1)),
        ],
        compiler_params=pltpu.CompilerParams(
            collective_id=0, has_side_effects=True, vmem_limit_bytes=63 << 20),
    )(tokens, w_gate, w_up, w_down)


def by_collectives(tokens, w_gate, w_up, w_down):
    columns = w_gate.shape[1]
    paired_weights = jnp.concatenate([w_gate, w_up], axis=1)
    partial_terms = jnp.dot(
        lax.all_gather(tokens, "mp", axis=0, tiled=True), paired_weights, preferred_element_type=F32)
    summed = lax.psum_scatter(partial_terms, ("dp", "guide"), scatter_dimension=0, tiled=True)
    hidden_share = (jax.nn.silu(summed[:, :columns]) * summed[:, columns:]).astype(BF16)
    hidden = lax.all_gather(hidden_share, ("dp", "guide"), axis=0, tiled=True)
    output_share = lax.psum_scatter(
        jnp.dot(hidden, w_down, preferred_element_type=F32), "mp", scatter_dimension=0, tiled=True)
    return output_share.astype(BF16)


def solution(mesh):
    mp, dp = mesh.shape["mp"], mesh.shape["dp"]

    def per_device(tokens, w_gate, w_up, w_down):
        whole_chunks = w_gate.shape[1] % (2 * WIDTH) == 0 and w_down.shape[1] % OUT_WIDTH == 0
        if whole_chunks and tokens.shape[0] % 8 == 0 and tokens.shape[0] * mp % (16 * dp) == 0:
            return fused(mp, dp, tokens, w_gate, w_up, w_down)
        return by_collectives(tokens, w_gate, w_up, w_down)

    placed = (
        P(("groups", "mp"), ("dp", "guide")),
        P(("dp", "guide"), "mp"),
        P(("dp", "guide"), "mp"),
        P("mp", ("dp", "guide")),
    )
    return jax.shard_map(
        per_device, mesh=mesh, in_specs=placed,
        out_specs=P(("groups", "mp"), ("dp", "guide")), check_vma=False)
```

time: 123 us -> 46.5 us (0.38)
  waiting for transfers between devices: 61.1 us -> 0 us
  Pallas kernels: 0 us -> 44.8 us
  blocking collectives: 24 us -> 0 us
  matrix products: 21.4 us -> 0 us
  between operations: 13.4 us -> 0.01 us
  other arithmetic: 2.76 us -> 0 us
  local copies, waits for them, and re-layouts: 0 us -> 1.54 us
    reduce_scatter x2 -> x0, waiting for transfers between devices: 61 us -> none  [the longest x1 37.2 us: per_device(): lax.psum_scatter(partial_terms, ('dp', 'guide'), scatter_dimension=0, til...]
    pallas_call x0 -> x1, Pallas kernels: none -> 44.8 us  [fused(): pl.pallas_call(functools.partial(kernel, mp, dp), out_shape=jax.ShapeDtyp...]
    all_gather x2 -> x0, blocking collectives: 24 us -> none  [the longest x1 16.5 us: per_device(): lax.all_gather(tokens, 'mp', axis=0, tiled=True)]
    dot_general x2 -> x0, matrix products: 21.4 us -> none  [the longest x1 12.8 us: per_device(): jnp.dot(lax.all_gather(tokens, 'mp', axis=0, tiled=True), paired_weights,...]
    convert_element_type x2 -> x0, other arithmetic: 2.76 us -> none  [the longest x1 1.58 us: per_device(): return output_share.astype(jnp.bfloat16)]
    unnamed x0 -> x1, local copies, waits for them, and re-layouts: none -> 1.54 us
  transfers between devices with their start and end apart: 2 -> 0, of which waited for: 2 -> 0; matrix products, arithmetic and copies ran while one was open for 0% -> 0% of each run, Pallas kernels for 0% -> 0%
where the time goes in v1:
time: 46.5 us; the launch traced here: 46.4 us
  Pallas kernels  44.8 us (96%)
  local copies, waits for them, and re-layouts  1.54 us (3%)
    pallas_call x1, Pallas kernels, fused(): pl.pallas_call(functools.partial(kernel, mp, dp), out_shape=jax.ShapeDtyp...  44.8 us
    unnamed x1, local copies, waits for them, and re-layouts  1.54 us

profile of v1, /device:TPU:0, one launch (start us, length us, event | category | flops | bytes accessed | tf_op | source)
XLA Modules:
  0.0 46.4 jit_solution(3582461873000124079)
XLA Ops:
  0.0 44.8 %shard_map.46 = bf16[24,2048]{1,0:T(8,128)(2,1)} custom-call(bf16[24,2048]{1,0:T(8,128)(2,1)} %tokens.1, bf16[2048,3584]{1,0:T(8,128)(2,1)} %w_gate.1, bf16[2048,3584]{1,0:T(8,128)(2,1)} %w_up.1, bf16[3584,2048]{1,0:T(8,128)(2,1)} %w_down.1), custom_call_target="tpu_custom_call" | custom-call | tf_op jit(solution)/shard_map/pallas_call | solution.py:197
  44.8 1.5 %copy.6 = bf16[24,2048]{1,0:T(8,128)(2,1)} copy(bf16[24,2048]{1,0:T(8,128)(2,1)} %shard_map.46) | data formatting | bytes 196608

commit v2 on v1

v2 whole, which is shorter than its diff:
```python
import functools

import jax
import jax.numpy as jnp
from jax import lax
from jax.experimental import pallas as pl
from jax.experimental.pallas import tpu as pltpu
from jax.sharding import PartitionSpec as P

MESH = pl.DeviceIdType.MESH
F32, BF16 = jnp.float32, jnp.bfloat16
WIDTH = 256
OUT_WIDTH = 512


def kernel(mp, dp, tokens, w_gate, w_up, w_down, out, *scratch):
    (gate_v, up_v, down_v, tok_in, tok_f, tok, sum1_out, sum1_in, kept, sum2_out, sum2_in,
     hid, part, out_send, out_recv,
     w_sem, down_sem, tok_own, tok_s, tok_r, s1_s, s1_r, s2_s, s2_r, hx_s, hx_r, hp_s, hp_r, c_s, c_r) = scratch
    m, d, g = lax.axis_index("mp"), lax.axis_index("dp"), lax.axis_index("guide")
    rows, depth = tokens.shape
    n_half = gate_v.shape[0] // 2
    n_out = down_v.shape[0]
    share = rows * mp // dp
    other = 1 - g
    far = mp // 2
    ways = ((0, 1), (1, mp - 1))

    def weights(side, c):
        half = other if side == 0 else g
        cols = pl.ds(pl.multiple_of((half * n_half + c) * WIDTH, WIDTH), WIDTH)
        slot = side * n_half + c
        return (pltpu.make_async_copy(w_gate.at[:, cols], gate_v.at[slot], w_sem.at[0, slot]),
                pltpu.make_async_copy(w_up.at[:, cols], up_v.at[slot], w_sem.at[1, slot]))

    def downs(n):
        return pltpu.make_async_copy(
            w_down.at[:, pl.ds(pl.multiple_of(n * OUT_WIDTH, OUT_WIDTH), OUT_WIDTH)], down_v.at[n], down_sem.at[n])

    def halves(way, wide):
        return pl.ds(way * (wide // 2), wide // 2)

    own = pltpu.make_async_copy(tokens, tok_in.at[m], tok_own)
    own.start()
    for side in range(2):
        for copy in weights(side, 0):
            copy.start()

    barrier = pltpu.get_barrier_semaphore()
    for _, j in ways:
        pl.semaphore_signal(barrier, inc=1, device_id={"mp": lax.rem(m + j, mp)}, device_id_type=MESH)
    for j in range(1, dp):
        pl.semaphore_signal(barrier, inc=1, device_id={"dp": lax.rem(d + j, dp)}, device_id_type=MESH)
    pl.semaphore_signal(barrier, inc=1, device_id={"guide": other}, device_id_type=MESH)
    pl.semaphore_wait(barrier, 2 + dp)

    def tok_copy(way, s):
        j = ways[way][1]
        block = tok_in.at[lax.rem(m + (s - 1) * (mp - j), mp)]
        if s == far:
            block = block.at[:, halves(way, depth)]
        return pltpu.make_async_remote_copy(
            src_ref=block, dst_ref=block, send_sem=tok_s.at[way, s - 1], recv_sem=tok_r.at[way, s - 1],
            device_id={"mp": lax.rem(m + j, mp)}, device_id_type=MESH)

    def widen(q):
        tok_f[pl.ds(pl.multiple_of(q * rows, 8), rows), :] = tok_in[q].astype(F32)

    own.wait()
    for way, _ in ways:
        tok_copy(way, 1).start()

    @pl.loop(1, n_half)
    def _(c):
        for side in range(2):
            for copy in weights(side, c):
                copy.start()

    @pl.loop(0, n_out)
    def _(n):
        downs(n).start()

    widen(m)
    for s in range(1, far + 1):
        for way, _ in ways:
            tok_copy(way, s).wait_recv()
            if s < far:
                tok_copy(way, s + 1).start()
        if s < far:
            for _, j in ways:
                widen(lax.rem(m + s * (mp - j), mp))
    widen(lax.rem(m + far, mp))
    tok[...] = tok_f[...].astype(BF16)

    def s1_copy(c):
        return pltpu.make_async_remote_copy(
            src_ref=sum1_out.at[c], dst_ref=sum1_in.at[c], send_sem=s1_s.at[c], recv_sem=s1_r.at[c],
            device_id={"guide": other}, device_id_type=MESH)

    def s2_copy(c, j):
        return pltpu.make_async_remote_copy(
            src_ref=sum2_out.at[c, j - 1], dst_ref=sum2_in.at[c, j - 1],
            send_sem=s2_s.at[c, j - 1], recv_sem=s2_r.at[c, j - 1],
            device_id={"dp": lax.rem(d + j, dp)}, device_id_type=MESH)

    def rows_of(b):
        return pl.ds(pl.multiple_of(b * share, 16), share)

    def pair_sum(c):
        s1_copy(c).wait_recv()
        for j in range(1, dp):
            b = rows_of(lax.rem(d + j, dp))
            for k in range(2):
                sum2_out[c, j - 1, k] = (kept[c, k, b, :] + sum1_in[c, k, b, :]).astype(BF16)
            s2_copy(c, j).start()

    @pl.loop(0, n_half)
    def _(c):
        for copy in weights(0, c):
            copy.wait()
        sum1_out[c, 0] = jnp.dot(tok[...], gate_v[c], preferred_element_type=F32)
        sum1_out[c, 1] = jnp.dot(tok[...], up_v[c], preferred_element_type=F32)
        s1_copy(c).start()
        for copy in weights(1, c):
            copy.wait()
        kept[c, 0] = jnp.dot(tok[...], gate_v[n_half + c], preferred_element_type=F32)
        kept[c, 1] = jnp.dot(tok[...], up_v[n_half + c], preferred_element_type=F32)

        @pl.when(c > 0)
        def _():
            pair_sum(c - 1)

    pair_sum(n_half - 1)

    def block(b, half, c):
        return hid.at[rows_of(b), pl.ds(pl.multiple_of((half * n_half + c) * WIDTH, WIDTH), WIDTH)]

    def hx_copy(c, j):
        return pltpu.make_async_remote_copy(
            src_ref=block(d, g, c), dst_ref=block(d, g, c), send_sem=hx_s.at[c, j - 1], recv_sem=hx_r.at[c, j - 1],
            device_id={"dp": lax.rem(d + j, dp)}, device_id_type=MESH)

    def hp_copy(c, j):
        b = block(lax.rem(d + dp - j, dp), g, c)
        return pltpu.make_async_remote_copy(
            src_ref=b, dst_ref=b, send_sem=hp_s.at[c, j], recv_sem=hp_r.at[c, j],
            device_id={"guide": other}, device_id_type=MESH)

    @pl.loop(0, n_half)
    def _(c):
        gate, up = [kept[c, k, rows_of(d), :] + sum1_in[c, k, rows_of(d), :] for k in range(2)]
        for j in range(1, dp):
            s2_copy(c, j).wait_recv()
            gate = gate + sum2_in[c, j - 1, 0].astype(F32)
            up = up + sum2_in[c, j - 1, 1].astype(F32)
        block(d, g, c)[...] = (gate / (1.0 + jnp.exp(-gate)) * up).astype(BF16)
        for j in range(1, dp):
            hx_copy(c, j).start()
        hp_copy(c, 0).start()

    @pl.loop(0, n_half)
    def _(c):
        for j in range(1, dp):
            hx_copy(c, j).wait_recv()
            hp_copy(c, j).start()

    @pl.loop(0, n_half)
    def _(c):
        for j in range(dp):
            hp_copy(c, j).wait_recv()

    def c_copy(n, way, s):
        cols = halves(way, OUT_WIDTH) if s == far else pl.ds(0, OUT_WIDTH)
        return pltpu.make_async_remote_copy(
            src_ref=out_send.at[n, way, s - 1, :, cols], dst_ref=out_recv.at[n, way, s - 1, :, cols],
            send_sem=c_s.at[n, way, s - 1], recv_sem=c_r.at[n, way, s - 1],
            device_id={"mp": lax.rem(m + ways[way][1], mp)}, device_id_type=MESH)

    def mine(n, way, s, cols):
        q = lax.rem(m + s * ways[way][1], mp)
        return part[n, pl.ds(pl.multiple_of(q * rows, 8), rows), cols]

    def pass_on(n):
        for s in range(far - 1, 0, -1):
            for way, _ in ways:
                c_copy(n, way, s + 1).wait_recv()
                for h in range(2):
                    cols = halves(h, OUT_WIDTH)
                    term = mine(n, way, s, cols)
                    if s + 1 < far or h == way:
                        term = term + out_recv[n, way, s, :, cols].astype(F32)
                    out_send[n, way, s - 1, :, cols] = term.astype(BF16)
                c_copy(n, way, s).start()

    @pl.loop(0, n_out)
    def _(n):
        downs(n).wait()
        part[n] = jnp.dot(hid[...], down_v[n], preferred_element_type=F32)
        for way, _ in ways:
            cols = halves(way, OUT_WIDTH)
            out_send[n, way, far - 1, :, cols] = mine(n, way, far, cols).astype(BF16)
            c_copy(n, way, far).start()

        @pl.when(n > 0)
        def _():
            pass_on(n - 1)

    pass_on(n_out - 1)
    for n in range(n_out):
        acc = mine(n, 0, 0, pl.ds(0, OUT_WIDTH))
        for way, _ in ways:
            c_copy(n, way, 1).wait_recv()
            acc = acc + out_recv[n, way, 0].astype(F32)
        out[:, n * OUT_WIDTH:(n + 1) * OUT_WIDTH] = acc.astype(BF16)

    for way, _ in ways:
        for s in range(1, far + 1):
            tok_copy(way, s).wait_send()

    @pl.loop(0, n_half)
    def _(c):
        s1_copy(c).wait_send()
        for j in range(1, dp):
            s2_copy(c, j).wait_send()
            hx_copy(c, j).wait_send()
        for j in range(dp):
            hp_copy(c, j).wait_send()

    @pl.loop(0, n_out)
    def _(n):
        for way, _ in ways:
            for s in range(1, far + 1):
                c_copy(n, way, s).wait_send()


def fused(mp, dp, tokens, w_gate, w_up, w_down):
    rows, depth = tokens.shape
    cols, wide = w_gate.shape[1], w_down.shape[1]
    nc, nh, no = cols // WIDTH, cols // WIDTH // 2, wide // OUT_WIDTH
    full, share, far = rows * mp, rows * mp // dp, mp // 2
    dma = pltpu.SemaphoreType.DMA
    any_, vmem = pl.BlockSpec(memory_space=pl.ANY), pl.BlockSpec(memory_space=pltpu.VMEM)
    return pl.pallas_call(
        functools.partial(kernel, mp, dp),
        out_shape=jax.ShapeDtypeStruct((rows, wide), BF16),
        in_specs=[any_] * 4,
        out_specs=vmem,
        scratch_shapes=[
            pltpu.VMEM((nc, depth, WIDTH), BF16),
            pltpu.VMEM((nc, depth, WIDTH), BF16),
            pltpu.VMEM((no, cols, OUT_WIDTH), BF16),
            pltpu.VMEM((mp, rows, depth), BF16),
            pltpu.VMEM((full, depth), F32),
            pltpu.VMEM((full, depth), BF16),
            pltpu.VMEM((nh, 2, full, WIDTH), F32),
            pltpu.VMEM((nh, 2, full, WIDTH), F32),
            pltpu.VMEM((nh, 2, full, WIDTH), F32),
            pltpu.VMEM((nh, dp - 1, 2, share, WIDTH), BF16),
            pltpu.VMEM((nh, dp - 1, 2, share, WIDTH), BF16),
            pltpu.VMEM((full, cols), BF16),
            pltpu.VMEM((no, full, OUT_WIDTH), F32),
            pltpu.VMEM((no, 2, far, rows, OUT_WIDTH), BF16),
            pltpu.VMEM((no, 2, far, rows, OUT_WIDTH), BF16),
            dma((2, nc)), dma((no,)), dma, dma((2, far)), dma((2, far)),
            dma((nh,)), dma((nh,)), dma((nh, dp - 1)), dma((nh, dp - 1)),
            dma((nh, dp - 1)), dma((nh, dp - 1)), dma((nh, dp)), dma((nh, dp)),
            dma((no, 2, far)), dma((no, 2, far)),
        ],
        compiler_params=pltpu.CompilerParams(
            collective_id=0, has_side_effects=True, vmem_limit_bytes=63 << 20),
    )(tokens, w_gate, w_up, w_down)


def by_collectives(tokens, w_gate, w_up, w_down):
    columns = w_gate.shape[1]
    paired_weights = jnp.concatenate([w_gate, w_up], axis=1)
    partial_terms = jnp.dot(
        lax.all_gather(tokens, "mp", axis=0, tiled=True), paired_weights, preferred_element_type=F32)
    summed = lax.psum_scatter(partial_terms, ("dp", "guide"), scatter_dimension=0, tiled=True)
    hidden_share = (jax.nn.silu(summed[:, :columns]) * summed[:, columns:]).astype(BF16)
    hidden = lax.all_gather(hidden_share, ("dp", "guide"), axis=0, tiled=True)
    output_share = lax.psum_scatter(
        jnp.dot(hidden, w_down, preferred_element_type=F32), "mp", scatter_dimension=0, tiled=True)
    return output_share.astype(BF16)


def solution(mesh):
    mp, dp = mesh.shape["mp"], mesh.shape["dp"]

    def per_device(tokens, w_gate, w_up, w_down):
        whole_chunks = w_gate.shape[1] % (2 * WIDTH) == 0 and w_down.shape[1] % OUT_WIDTH == 0
        if whole_chunks and mp % 2 == 0 and mp > 2 and tokens.shape[0] % 8 == 0 and tokens.shape[0] * mp % (16 * dp) == 0:
            return fused(mp, dp, tokens, w_gate, w_up, w_down)
        return by_collectives(tokens, w_gate, w_up, w_down)

    placed = (
        P(("groups", "mp"), ("dp", "guide")),
        P(("dp", "guide"), "mp"),
        P(("dp", "guide"), "mp"),
        P("mp", ("dp", "guide")),
    )
    return jax.shard_map(
        per_device, mesh=mesh, in_specs=placed,
        out_specs=P(("groups", "mp"), ("dp", "guide")), check_vma=False)
```

time: 46.5 us -> 48.5 us (1.043)
  Pallas kernels: 44.8 us -> 46.8 us
    pallas_call x1, Pallas kernels: 44.8 us -> 46.8 us  [fused(): pl.pallas_call(functools.partial(kernel, mp, dp), out_shape=jax.ShapeDtyp...]
where the time goes in v2:
time: 48.5 us; the launch traced here: 48.4 us
  Pallas kernels  46.8 us (96%)
  local copies, waits for them, and re-layouts  1.54 us (3%)
    pallas_call x1, Pallas kernels, fused(): pl.pallas_call(functools.partial(kernel, mp, dp), out_shape=jax.ShapeDtyp...  46.8 us
    unnamed x1, local copies, waits for them, and re-layouts  1.54 us

profile of v2, /device:TPU:0, one launch (start us, length us, event | category | flops | bytes accessed | tf_op | source)
XLA Modules:
  0.0 48.4 jit_solution(3183491740973135917)
XLA Ops:
  0.0 46.8 %shard_map.46 = bf16[24,2048]{1,0:T(8,128)(2,1)} custom-call(bf16[24,2048]{1,0:T(8,128)(2,1)} %tokens.1, bf16[2048,3584]{1,0:T(8,128)(2,1)} %w_gate.1, bf16[2048,3584]{1,0:T(8,128)(2,1)} %w_up.1, bf16[3584,2048]{1,0:T(8,128)(2,1)} %w_down.1), custom_call_target="tpu_custom_call" | custom-call | tf_op jit(solution)/shard_map/pallas_call | solution.py:243
  46.8 1.5 %copy.6 = bf16[24,2048]{1,0:T(8,128)(2,1)} copy(bf16[24,2048]{1,0:T(8,128)(2,1)} %shard_map.46) | data formatting | bytes 196608

commit v3 on v1

--- a/solution.py
+++ b/solution.py
@@ -14,22 +14,25 @@
 
 
 def kernel(mp, dp, tokens, w_gate, w_up, w_down, out, *scratch):
-    (gate_v, up_v, down_v, tok_in, tok_f, tok, sum1_out, sum1_in, total, kept, sum2_out, sum2_in,
-     hid, part, out_kept, out_send, out_recv,
+    (gate_v, up_v, down_v, tok_in, tok_f, tok, sum1_out, sum1_in, kept, sum2_out, sum2_in,
+     hid, part, out_send, out_recv,
      w_sem, down_sem, tok_own, tok_s, tok_r, s1_s, s1_r, s2_s, s2_r, hx_s, hx_r, hp_s, hp_r, c_s, c_r) = scratch
     m, d, g = lax.axis_index("mp"), lax.axis_index("dp"), lax.axis_index("guide")
-    rows = tokens.shape[0]
-    n_half = gate_v.shape[0] // 2
+    rows, depth = tokens.shape
+    n_half = gate_v.shape[2] // WIDTH
     n_out = down_v.shape[0]
     share = rows * mp // dp
     other = 1 - g
+    piece = depth // 2
+    peers = sorted(range(1, mp), key=lambda j: -min(j, mp - j))
 
     def weights(side, c):
         half = other if side == 0 else g
         cols = pl.ds(pl.multiple_of((half * n_half + c) * WIDTH, WIDTH), WIDTH)
         slot = side * n_half + c
-        return (pltpu.make_async_copy(w_gate.at[:, cols], gate_v.at[slot], w_sem.at[0, slot]),
-                pltpu.make_async_copy(w_up.at[:, cols], up_v.at[slot], w_sem.at[1, slot]))
+        to = pl.ds(pl.multiple_of(c * WIDTH, WIDTH), WIDTH)
+        return (pltpu.make_async_copy(w_gate.at[:, cols], gate_v.at[side, :, to], w_sem.at[0, slot]),
+                pltpu.make_async_copy(w_up.at[:, cols], up_v.at[side, :, to], w_sem.at[1, slot]))
 
     def downs(n):
         return pltpu.make_async_copy(
@@ -55,32 +58,42 @@
     pl.semaphore_signal(barrier, inc=1, device_id={"guide": other}, device_id_type=MESH)
     pl.semaphore_wait(barrier, mp + dp - 1)
 
-    def tok_copy(j):
-        return pltpu.make_async_remote_copy(
-            src_ref=tokens, dst_ref=tok_in.at[m], send_sem=tok_s.at[j - 1], recv_sem=tok_r.at[j - 1],
+    def tok_copy(p, j):
+        cols = pl.ds(p * piece, piece)
+        return pltpu.make_async_remote_copy(
+            src_ref=tokens.at[:, cols], dst_ref=tok_in.at[m, :, cols],
+            send_sem=tok_s.at[p, j - 1], recv_sem=tok_r.at[p, j - 1],
             device_id={"mp": lax.rem(m + j, mp)}, device_id_type=MESH)
 
-    for j in range(mp - 1, 0, -1):
-        tok_copy(j).start()
+    for p in range(2):
+        for j in peers:
+            tok_copy(p, j).start()
     own.wait()
-    for j in range(1, mp):
-        tok_copy(j).wait_recv()
-    for q in range(mp):
-        tok_f[q * rows:(q + 1) * rows, :] = tok_in[q].astype(F32)
-    tok[...] = tok_f[...].astype(BF16)
+
+    def gather(p):
+        cols = slice(p * piece, (p + 1) * piece)
+        for j in range(1, mp):
+            tok_copy(p, j).wait_recv()
+        for q in range(mp):
+            tok_f[q * rows:(q + 1) * rows, :] = tok_in[q, :, cols].astype(F32)
+        tok[:, cols] = tok_f[...].astype(BF16)
+
+    gather(0)
+    for side, sums in ((0, sum1_out), (1, kept)):
+        @pl.loop(0, n_half)
+        def _(c):
+            for copy in weights(side, c):
+                copy.wait()
+        for k, held in ((0, gate_v), (1, up_v)):
+            value = jnp.dot(tok[:, :piece], held[side, :piece, :], preferred_element_type=F32)
+            for c in range(n_half):
+                sums[c, k] = value[:, c * WIDTH:(c + 1) * WIDTH]
+    gather(1)
 
     def s1_copy(c):
         return pltpu.make_async_remote_copy(
             src_ref=sum1_out.at[c], dst_ref=sum1_in.at[c], send_sem=s1_s.at[c], recv_sem=s1_r.at[c],
             device_id={"guide": other}, device_id_type=MESH)
-
-    @pl.loop(0, n_half)
-    def _(c):
-        for copy in weights(0, c):
-            copy.wait()
-        sum1_out[c, 0] = jnp.dot(tok[...], gate_v[c], preferred_element_type=F32).astype(BF16)
-        sum1_out[c, 1] = jnp.dot(tok[...], up_v[c], preferred_element_type=F32).astype(BF16)
-        s1_copy(c).start()
 
     def s2_copy(c, j):
         return pltpu.make_async_remote_copy(
@@ -91,20 +104,26 @@
     def rows_of(b):
         return pl.ds(pl.multiple_of(b * share, 16), share)
 
-    @pl.loop(0, n_half)
-    def _(c):
-        for copy in weights(1, c):
-            copy.wait()
-        total[0] = jnp.dot(tok[...], gate_v[n_half + c], preferred_element_type=F32)
-        total[1] = jnp.dot(tok[...], up_v[n_half + c], preferred_element_type=F32)
+    def pair_sum(c):
         s1_copy(c).wait_recv()
         for j in range(1, dp):
             b = rows_of(lax.rem(d + j, dp))
             for k in range(2):
-                sum2_out[c, j - 1, k] = (total[k, b, :] + sum1_in[c, k, b, :].astype(F32)).astype(BF16)
+                sum2_out[c, j - 1, k] = (kept[c, k, b, :] + sum1_in[c, k, b, :]).astype(BF16)
             s2_copy(c, j).start()
-        for k in range(2):
-            kept[c, k] = total[k, rows_of(d), :] + sum1_in[c, k, rows_of(d), :].astype(F32)
+
+    def finish(side, sums, c):
+        for k, held in ((0, gate_v), (1, up_v)):
+            sums[c, k] += jnp.dot(
+                tok[:, piece:], held[side, piece:, c * WIDTH:(c + 1) * WIDTH], preferred_element_type=F32)
+
+    for c in range(n_half):
+        finish(0, sum1_out, c)
+        s1_copy(c).start()
+        finish(1, kept, c)
+        if c > 0:
+            pair_sum(c - 1)
+    pair_sum(n_half - 1)
 
     def block(b, half, c):
         return hid.at[rows_of(b), pl.ds(pl.multiple_of((half * n_half + c) * WIDTH, WIDTH), WIDTH)]
@@ -122,10 +141,9 @@
 
     @pl.loop(0, n_half)
     def _(c):
+        gate, up = [kept[c, k, rows_of(d), :] + sum1_in[c, k, rows_of(d), :] for k in range(2)]
         for j in range(1, dp):
             s2_copy(c, j).wait_recv()
-        gate, up = kept[c, 0], kept[c, 1]
-        for j in range(1, dp):
             gate = gate + sum2_in[c, j - 1, 0].astype(F32)
             up = up + sum2_in[c, j - 1, 1].astype(F32)
         block(d, g, c)[...] = (gate / (1.0 + jnp.exp(-gate)) * up).astype(BF16)
@@ -153,24 +171,23 @@
     def out_rows(q):
         return pl.ds(pl.multiple_of(q * rows, 8), rows)
 
-    @pl.loop(0, n_out)
-    def _(n):
+    for n in range(n_out):
         downs(n).wait()
-        part[...] = jnp.dot(hid[...], down_v[n], preferred_element_type=F32)
-        for j in range(mp - 1, 0, -1):
-            out_send[n, j - 1] = part[out_rows(lax.rem(m + j, mp)), :].astype(BF16)
+        part[n] = jnp.dot(hid[...], down_v[n], preferred_element_type=F32)
+        for j in peers:
+            out_send[n, j - 1] = part[n, out_rows(lax.rem(m + j, mp)), :].astype(BF16)
             c_copy(n, j).start()
-        out_kept[n] = part[out_rows(m), :]
 
     for n in range(n_out):
-        acc = out_kept[n]
+        acc = part[n, out_rows(m), :]
         for j in range(1, mp):
             c_copy(n, j).wait_recv()
             acc = acc + out_recv[n, j - 1].astype(F32)
         out[:, n * OUT_WIDTH:(n + 1) * OUT_WIDTH] = acc.astype(BF16)
 
-    for j in range(1, mp):
-        tok_copy(j).wait_send()
+    for p in range(2):
+        for j in range(1, mp):
+            tok_copy(p, j).wait_send()
 
     @pl.loop(0, n_half)
     def _(c):
@@ -200,24 +217,22 @@
         in_specs=[any_] * 4,
         out_specs=vmem,
         scratch_shapes=[
-            pltpu.VMEM((nc, depth, WIDTH), BF16),
-            pltpu.VMEM((nc, depth, WIDTH), BF16),
+            pltpu.VMEM((2, depth, cols // 2), BF16),
+            pltpu.VMEM((2, depth, cols // 2), BF16),
             pltpu.VMEM((no, cols, OUT_WIDTH), BF16),
             pltpu.VMEM((mp, rows, depth), BF16),
-            pltpu.VMEM((full, depth), F32),
+            pltpu.VMEM((full, depth // 2), F32),
             pltpu.VMEM((full, depth), BF16),
-            pltpu.VMEM((nh, 2, full, WIDTH), BF16),
-            pltpu.VMEM((nh, 2, full, WIDTH), BF16),
-            pltpu.VMEM((2, full, WIDTH), F32),
-            pltpu.VMEM((nh, 2, share, WIDTH), F32),
+            pltpu.VMEM((nh, 2, full, WIDTH), F32),
+            pltpu.VMEM((nh, 2, full, WIDTH), F32),
+            pltpu.VMEM((nh, 2, full, WIDTH), F32),
             pltpu.VMEM((nh, dp - 1, 2, share, WIDTH), BF16),
             pltpu.VMEM((nh, dp - 1, 2, share, WIDTH), BF16),
             pltpu.VMEM((full, cols), BF16),
-            pltpu.VMEM((full, OUT_WIDTH), F32),
-            pltpu.VMEM((no, rows, OUT_WIDTH), F32),
+            pltpu.VMEM((no, full, OUT_WIDTH), F32),
             pltpu.VMEM((no, mp - 1, rows, OUT_WIDTH), BF16),
             pltpu.VMEM((no, mp - 1, rows, OUT_WIDTH), BF16),
-            dma((2, nc)), dma((no,)), dma, dma((mp - 1,)), dma((mp - 1,)),
+            dma((2, nc)), dma((no,)), dma, dma((2, mp - 1)), dma((2, mp - 1)),
             dma((nh,)), dma((nh,)), dma((nh, dp - 1)), dma((nh, dp - 1)),
             dma((nh, dp - 1)), dma((nh, dp - 1)), dma((nh, dp)), dma((nh, dp)),
             dma((no, mp - 1)), dma((no, mp - 1)),
@@ -245,7 +260,7 @@
 
     def per_device(tokens, w_gate, w_up, w_down):
         whole_chunks = w_gate.shape[1] % (2 * WIDTH) == 0 and w_down.shape[1] % OUT_WIDTH == 0
-        if whole_chunks and tokens.shape[0] % 8 == 0 and tokens.shape[0] * mp % (16 * dp) == 0:
+        if whole_chunks and mp > 1 and tokens.shape[1] % 512 == 0 and tokens.shape[0] % 8 == 0 and tokens.shape[0] * mp % (16 * dp) == 0:
             return fused(mp, dp, tokens, w_gate, w_up, w_down)
         return by_collectives(tokens, w_gate, w_up, w_down)
 

time: 46.5 us -> 46.3 us (level)
  no operation moved by 1% of the time
where the time goes in v3:
time: 46.3 us; the launch traced here: 46.1 us
  Pallas kernels  44.6 us (96%)
  local copies, waits for them, and re-layouts  1.54 us (3%)
    pallas_call x1, Pallas kernels, fused(): pl.pallas_call(functools.partial(kernel, mp, dp), out_shape=jax.ShapeDtyp...  44.6 us
    unnamed x1, local copies, waits for them, and re-layouts  1.54 us

profile of v3, /device:TPU:0, one launch (start us, length us, event | category | flops | bytes accessed | tf_op | source)
XLA Modules:
  0.0 46.1 jit_solution(6493201565154276053)
XLA Ops:
  0.0 44.6 %shard_map.46 = bf16[24,2048]{1,0:T(8,128)(2,1)} custom-call(bf16[24,2048]{1,0:T(8,128)(2,1)} %tokens.1, bf16[2048,3584]{1,0:T(8,128)(2,1)} %w_gate.1, bf16[2048,3584]{1,0:T(8,128)(2,1)} %w_up.1, bf16[3584,2048]{1,0:T(8,128)(2,1)} %w_down.1), custom_call_target="tpu_custom_call" | custom-call | tf_op jit(solution)/shard_map/pallas_call | solution.py:214
  44.6 1.5 %copy.6 = bf16[24,2048]{1,0:T(8,128)(2,1)} copy(bf16[24,2048]{1,0:T(8,128)(2,1)} %shard_map.46) | data formatting | bytes 196608

commit v4 on v3

--- a/solution.py
+++ b/solution.py
@@ -24,7 +24,7 @@
     share = rows * mp // dp
     other = 1 - g
     piece = depth // 2
-    peers = sorted(range(1, mp), key=lambda j: -min(j, mp - j))
+    peers = range(mp - 1, 0, -1)
 
     def weights(side, c):
         half = other if side == 0 else g
@@ -171,7 +171,8 @@
     def out_rows(q):
         return pl.ds(pl.multiple_of(q * rows, 8), rows)
 
-    for n in range(n_out):
+    @pl.loop(0, n_out)
+    def _(n):
         downs(n).wait()
         part[n] = jnp.dot(hid[...], down_v[n], preferred_element_type=F32)
         for j in peers:

time: 46.3 us -> 47.3 us (1.022)
  Pallas kernels: 44.6 us -> 45.6 us
    pallas_call x1, Pallas kernels: 44.6 us -> 45.6 us  [fused(): pl.pallas_call(functools.partial(kernel, mp, dp), out_shape=jax.ShapeDtyp...]
where the time goes in v4:
time: 47.3 us; the launch traced here: 47.2 us
  Pallas kernels  45.6 us (96%)
  local copies, waits for them, and re-layouts  1.54 us (3%)
    pallas_call x1, Pallas kernels, fused(): pl.pallas_call(functools.partial(kernel, mp, dp), out_shape=jax.ShapeDtyp...  45.6 us
    unnamed x1, local copies, waits for them, and re-layouts  1.54 us

profile of v4, /device:TPU:0, one launch (start us, length us, event | category | flops | bytes accessed | tf_op | source)
XLA Modules:
  0.0 47.2 jit_solution(8413255872384816820)
XLA Ops:
  0.0 45.6 %shard_map.46 = bf16[24,2048]{1,0:T(8,128)(2,1)} custom-call(bf16[24,2048]{1,0:T(8,128)(2,1)} %tokens.1, bf16[2048,3584]{1,0:T(8,128)(2,1)} %w_gate.1, bf16[2048,3584]{1,0:T(8,128)(2,1)} %w_up.1, bf16[3584,2048]{1,0:T(8,128)(2,1)} %w_down.1), custom_call_target="tpu_custom_call" | custom-call | tf_op jit(solution)/shard_map/pallas_call | solution.py:215
  45.6 1.5 %copy.6 = bf16[24,2048]{1,0:T(8,128)(2,1)} copy(bf16[24,2048]{1,0:T(8,128)(2,1)} %shard_map.46) | data formatting | bytes 196608
